TPU v7x, 32 devices: a whole 2x2x4 slice. The times are simulated.
32 devices in a mesh: blk: 8 (over z, x), uly: 4 (over y, core).
Axes of the slice: x: 2, y: 2, z: 4, core: 2. Of those that a mesh axis runs over, the one named last changes fastest.
Arguments:
- query_projection: bfloat16 [4096, 4096], P(('blk', 'uly')), may hold values from -4.5 to 4.5
- key_projection: bfloat16 [4096, 512], P(('blk', 'uly')), may hold values from -4.5 to 4.5
- value_projection: bfloat16 [4096, 512], P(('blk', 'uly')), may hold values from -6 to 6
- doc_start: int32 [4096], P('blk'), may hold values from 0 to 4095, as said below
Outputs:
- attn: bfloat16 [4096, 4096], P(('blk', 'uly'))
Inputs may be any that keep to these rules, and one draw needn't show every extreme that they name: Documents are contiguous runs of positions: doc_start[0] = 0, doc_start never falls, doc_start[i] <= i, and doc_start[doc_start[i]] = doc_start[i]. Every document has at most 1024 positions; the first has exactly 1024, and another of exactly 1024 begins strictly inside a block of 512 positions. The last position begins a document of its own.
All inputs are finite; a program needn't handle non-finite values.
Results may differ from a plain program's by a relative error of at most 0.0031.
Values may be sent and summed in bfloat16 or wider, within the bound.
A program may use at most 64 MiB of HBM per device.

v0:
```python
import jax
import jax.numpy as jnp
from jax import lax
from jax.sharding import PartitionSpec as P

HEAD_WIDTH = 128
CYCLE_STEPS = 2
POSITION_GROUP = 512
masked_score = -1e30


def from_behind(block, axis, distance):
    devices = range(lax.axis_size(axis))
    route = [(i - distance, i) for i in devices if i - distance in devices]
    return lax.ppermute(block, axis, route)


def local(query_projection, key_projection, value_projection, doc_start):
    width = lax.axis_size("uly")
    tokens_dev = query_projection.shape[0]
    kv_heads = key_projection.shape[1] // HEAD_WIDTH
    repeats = max(1, width // kv_heads)

    def widen_heads(source):
        split_heads = source.reshape(tokens_dev, kv_heads, 1, HEAD_WIDTH)
        copies = jnp.broadcast_to(split_heads, (tokens_dev, kv_heads, repeats, HEAD_WIDTH))
        return copies.reshape(tokens_dev, kv_heads * repeats * HEAD_WIDTH)

    query_rows = lax.all_to_all(query_projection, "uly", split_axis=1, concat_axis=0, tiled=True)
    key_rows, value_rows = (
        lax.all_to_all(widen_heads(key_projection), "uly", split_axis=1, concat_axis=0, tiled=True),
        lax.all_to_all(
            widen_heads(value_projection), "uly", split_axis=1, concat_axis=0, tiled=True
        ),
    )
    row_count = query_rows.shape[0]
    local_kv = key_rows.shape[1] // HEAD_WIDTH
    local_q = query_rows.shape[1] // HEAD_WIDTH
    query_group_width = local_q // local_kv
    earlier = []
    for step in range(CYCLE_STEPS):
        earlier.insert(0, from_behind((key_rows, value_rows), "blk", step + 1))
    joined_keys = jnp.concatenate([piece[0] for piece in earlier] + [key_rows], axis=0).reshape(
        -1, local_kv, HEAD_WIDTH
    )
    joined_values = jnp.concatenate([piece[1] for piece in earlier] + [value_rows], axis=0).reshape(
        -1, local_kv, HEAD_WIDTH
    )
    lead = CYCLE_STEPS * row_count
    base = lax.axis_index("blk") * row_count
    anchor = base - lead
    query_heads = query_rows.reshape(row_count, local_kv, query_group_width, HEAD_WIDTH)
    score_scale = HEAD_WIDTH ** (-0.5)

    def one_tile(index):
        start = index * POSITION_GROUP
        query_tile = lax.dynamic_slice_in_dim(query_heads, start, POSITION_GROUP, 0)
        starts = lax.dynamic_slice_in_dim(doc_start, start, POSITION_GROUP, 0)
        query_places = base + start + jnp.arange(POSITION_GROUP, dtype=jnp.int32)
        first_tile = (jnp.min(starts) - anchor) // POSITION_GROUP
        last_tile = (lead + start) // POSITION_GROUP

        def add_tile(tile, carry):
            running_maximum, running_sum, running_output = carry
            key_start = tile * POSITION_GROUP
            key_tile = lax.dynamic_slice_in_dim(joined_keys, key_start, POSITION_GROUP, 0)
            value_tile = lax.dynamic_slice_in_dim(joined_values, key_start, POSITION_GROUP, 0)
            key_places = anchor + key_start + jnp.arange(POSITION_GROUP, dtype=jnp.int32)
            seen = (key_places[None, :] >= starts[:, None]) & (
                key_places[None, :] <= query_places[:, None]
            )
            seen = seen[:, None, None, :]
            scores = (
                jnp.einsum(
                    "tkgd,nkd->tkgn", query_tile, key_tile, preferred_element_type=jnp.float32
                )
                * score_scale
            )
            masked = jnp.where(seen, scores, masked_score)
            fresh = jnp.maximum(running_maximum, jnp.max(masked, axis=-1))
            factor = jnp.exp(running_maximum - fresh)
            exps = jnp.where(seen, jnp.exp(masked - fresh[..., None]), 0.0)
            running_sum = running_sum * factor + jnp.sum(exps, axis=-1)
            blended = jnp.einsum(
                "tkgn,nkd->tkgd",
                exps.astype(jnp.bfloat16),
                value_tile,
                preferred_element_type=jnp.float32,
            )
            running_output = running_output * factor[..., None] + blended
            return (fresh, running_sum, running_output)

        running_maximum = jnp.full(
            (POSITION_GROUP, local_kv, query_group_width), masked_score, jnp.float32
        )
        running_sum = jnp.zeros((POSITION_GROUP, local_kv, query_group_width), jnp.float32)
        running_output = jnp.zeros(
            (POSITION_GROUP, local_kv, query_group_width, HEAD_WIDTH), jnp.float32
        )
        running_maximum, running_sum, running_output = lax.fori_loop(
            first_tile, last_tile + 1, add_tile, (running_maximum, running_sum, running_output)
        )
        return (running_output / running_sum[..., None]).astype(jnp.bfloat16)

    outputs = lax.map(one_tile, jnp.arange(row_count // POSITION_GROUP, dtype=jnp.int32))
    attn = outputs.reshape(row_count, local_q * HEAD_WIDTH)
    return lax.all_to_all(attn, "uly", split_axis=0, concat_axis=1, tiled=True)


def solution(mesh):
    placed = (P(("blk", "uly"), None), P(("blk", "uly"), None), P(("blk", "uly"), None), P("blk"))
    return jax.shard_map(
        local, mesh=mesh, in_specs=placed, out_specs=P(("blk", "uly"), None), check_vma=False
    )
```

profile of v0, /device:TPU:18, one launch (start us, length us, event | category | flops | bytes accessed | tf_op | source)
XLA Modules:
  0.0 90.7 jit_solution(1253593889368224903)
XLA Ops:
  0.0 1.7 %copy.24 = bf16[128,512]{0,1:T(8,128)(2,1)} copy(bf16[128,512]{1,0:T(8,128)(2,1)} %param.8) | data formatting | bytes 262144 | tf_op args[2]
  1.7 3.3 %all-to-all-start.2 = ((bf16[128,4,128]{0,2,1:T(8,128)(2,1)}), bf16[128,4,128]{0,2,1:T(8,128)(2,1)S(1)}, u32[]{:S(2)}, u32[]{:S(2)}) async-start(bf16[128,4,128]{0,2,1:T(8,128)(2,1)} %bitcast.5), calls=%async_computation.2 | async-start | bytes 262144 | tf_op jit(solution)/shard_map/all_to_all | solution.py:32
  5.7 3.9 %all-to-all-done.2 = bf16[128,4,128]{0,2,1:T(8,128)(2,1)S(1)} async-done(((bf16[128,4,128]{0,2,1:T(8,128)(2,1)}), bf16[128,4,128]{0,2,1:T(8,128)(2,1)S(1)}, u32[]{:S(2)}, u32[]{:S(2)}) %all-to-all-start.2) | async-done | bytes 131104 | tf_op jit(solution)/shard_map/all_to_all | solution.py:32
  9.6 3.3 %all-to-all-start = ((bf16[128,4,128]{2,0,1:T(8,128)(2,1)}), bf16[128,4,128]{2,0,1:T(8,128)(2,1)S(1)}, u32[]{:S(2)}, u32[]{:S(2)}) async-start(bf16[128,4,128]{2,0,1:T(8,128)(2,1)} %copy_bitcast_fusion.1), calls=%async_computation | async-start | bytes 262144 | tf_op jit(solution)/shard_map/all_to_all | solution.py:31
  12.9 2.3 %copy.39 = bf16[16,4,8,1024]{3,2,0,1:T(8,128)(2,1)} copy(bf16[16,4,8,1024]{3,2,1,0:T(8,128)(2,1)} %bitcast.111) | data formatting | bytes 2097152 | tf_op jit(solution)/shard_map/all_to_all | solution.py:29
  15.2 2.3 %all-to-all-done = bf16[128,4,128]{2,0,1:T(8,128)(2,1)S(1)} async-done(((bf16[128,4,128]{2,0,1:T(8,128)(2,1)}), bf16[128,4,128]{2,0,1:T(8,128)(2,1)S(1)}, u32[]{:S(2)}, u32[]{:S(2)}) %all-to-all-start) | async-done | bytes 131104 | tf_op jit(solution)/shard_map/all_to_all | solution.py:31
  17.5 3.5 %all-to-all-start.1 = ((bf16[128,4,1024]{2,0,1:T(8,128)(2,1)}), bf16[128,4,1024]{2,0,1:T(8,128)(2,1)S(1)}, u32[]{:S(2)}, u32[]{:S(2)}) async-start(bf16[128,4,1024]{2,0,1:T(8,128)(2,1)} %bitcast.83), calls=%async_computation.1 | async-start | bytes 2097152 | tf_op jit(solution)/shard_map/all_to_all | solution.py:29
  21.2 3.5 %collective-permute-start.2 = (bf16[512,128]{1,0:T(8,128)(2,1)S(1)}, bf16[512,128]{1,0:T(8,128)(2,1)S(1)}, u32[]{:S(2)}, u32[]{:S(2)}) collective-permute-start(bf16[512,128]{1,0:T(8,128)(2,1)S(1)} %bitcast.116), channel_id=1, source_target_pairs={{0,8},{4,12},{8,16},{12,20},{16,24},{20,28},{1,9},{5,13},{9,17},{1... | collective-permute-start | bytes 393224 | tf_op jit(solution)/shard_map/ppermute | solution.py:15
  24.7 1.9 %collective-permute-start.3 = (bf16[512,128]{1,0:T(8,128)(2,1)S(1)}, bf16[512,128]{1,0:T(8,128)(2,1)S(1)}, u32[]{:S(2)}, u32[]{:S(2)}) collective-permute-start(bf16[512,128]{1,0:T(8,128)(2,1)S(1)} %bitcast.117), channel_id=1, source_target_pairs={{0,4},{4,8},{8,12},{12,16},{16,20},{20,24},{24,28},{1,5},{5,9},{9,... | collective-permute-start | bytes 393224 | tf_op jit(solution)/shard_map/ppermute | solution.py:15
  26.6 1.4 %reduce_min.10 = s32[]{:T(128)} reduce(s32[512]{0:T(512)} %param.9, s32[]{:T(128)} %constant.93.clone.1), dimensions={0}, to_apply=%region_0.1 | reduce | flops 511 | bytes 2056 | tf_op jit(solution)/shard_map/while/body/eval_jaxpr/reduce_min | solution.py:60
  28.7 1.9 %collective-permute-start = (bf16[512,128]{1,0:T(8,128)(2,1)S(1)}, bf16[512,128]{1,0:T(8,128)(2,1)S(1)}, u32[]{:S(2)}, u32[]{:S(2)}) collective-permute-start(bf16[512,128]{1,0:T(8,128)(2,1)S(1)} %bitcast.113), channel_id=1, source_target_pairs={{0,8},{4,12},{8,16},{12,20},{16,24},{20,28},{1,9},{5,13},{9,17},{1... | collective-permute-start | bytes 393224 | tf_op jit(solution)/shard_map/ppermute | solution.py:15
  30.6 2.1 %collective-permute-start.1 = (bf16[512,128]{1,0:T(8,128)(2,1)S(1)}, bf16[512,128]{1,0:T(8,128)(2,1)S(1)}, u32[]{:S(2)}, u32[]{:S(2)}) collective-permute-start(bf16[512,128]{1,0:T(8,128)(2,1)S(1)} %bitcast.114), channel_id=1, source_target_pairs={{0,4},{4,8},{8,12},{12,16},{16,20},{20,24},{24,28},{1,5},{5,9},{9,... | collective-permute-start | bytes 393224 | tf_op jit(solution)/shard_map/ppermute | solution.py:15
  32.8 0.8 maximum_bitcast_fusion.1
  33.5 2.6 %collective-permute-done = bf16[512,128]{1,0:T(8,128)(2,1)S(1)} collective-permute-done((bf16[512,128]{1,0:T(8,128)(2,1)S(1)}, bf16[512,128]{1,0:T(8,128)(2,1)S(1)}, u32[]{:S(2)}, u32[]{:S(2)}) %collective-permute-start) | collective-permute-done | bytes 131104 | tf_op jit(solution)/shard_map/ppermute | solution.py:15
  36.2 1.9 %collective-permute-done.1 = bf16[512,128]{1,0:T(8,128)(2,1)S(1)} collective-permute-done((bf16[512,128]{1,0:T(8,128)(2,1)S(1)}, bf16[512,128]{1,0:T(8,128)(2,1)S(1)}, u32[]{:S(2)}, u32[]{:S(2)}) %collective-permute-start.1) | collective-permute-done | bytes 131104 | tf_op jit(solution)/shard_map/ppermute | solution.py:15
  38.1 0.8 maximum_bitcast_fusion
  40.2 29.5 %while.24 = (s32[]{:T(128)}, f32[512,1,8]{0,2,1:T(8,128)S(1)}, f32[512,1,8]{0,2,1:T(8,128)}, f32[512,1,8,128]{0,3,2,1:T(8,128)S(1)}, s32[]{:T(128)}, /*index=5*/...) while((s32[]{:T(128)}, f32[512,1,8]{0,2,1:T(8,128)S(1)}, ...), condition=%wide.region_4.5_spmd.clone, body=%wide.region_1.4_spmd.clone.sunk | while | flops 1102853120 | bytes 32123144 | solution.py:100
  40.2 0.9 %compare_and_fusion.2 = pred[512,512]{0,1:T(8,128)(4,1)S(1)} fusion(s32[512]{0:T(512)S(1)} %get-tuple-element.256, s32[512]{0:T(512)} %get-tuple-element.295, s32[512]{0:T(512)S(1)} %get-tuple-element.257), kind=kLoop, calls=%fused_computation.12.clone.1 | loop fusion | flops 786432 | bytes 268288 | tf_op jit(solution)/shard_map/while/body/eval_jaxpr/while/body/and | solution.py:69
  41.1 2.4 %fusion.31 = (f32[512,8]{0,1:T(8,128)S(1)}, f32[512,512,8]{1,0,2:T(8,128)S(1)}) fusion(pred[512,512]{0,1:T(8,128)(4,1)S(1)} %compare_and_fusion.2, bf16[512,1,8,128]{3,0,2,1:T(8,128)(2,1)S(1)} %get-tuple-element.297, bf16[1536,1,128]{2,0,1:T(8,128)(2,1)} %get-tuple-element.296, s32[]{:T(128)S(6)} %select_n.64), kind=kOutput, calls=%fused_computation.3.clone.1 | convolution fusion | flops 543158272 | bytes 9846788 | tf_op jit(solution)/shard_map/while/body/eval_jaxpr/while/body/tkgd,nkd->tkgn/dot_general | solution.py:74
  43.6 3.7 %bitcast_add_fusion.5 = f32[512,1,8,128]{0,3,2,1:T(8,128)S(1)} fusion(f32[512,1,8,128]{0,3,2,1:T(8,128)S(1)} %get-tuple-element.279, f32[512,512,8]{1,0,2:T(8,128)S(1)} %get-tuple-element.260, f32[512,8]{0,1:T(8,128)S(1)} %bitcast.106, pred[512,512]{0,1:T(8,128)(4,1)S(1)} %compare_and_fusion.2, f32[512,8]{0,1:T(8,128)S(1)} %get-tuple-element.261, ...), kind=kOutput, calls=%fused_computation.9.clone.1 | convolution fusion | flops 548405248 | bytes 13008900 | tf_op jit(solution)/shard_map/while/body/eval_jaxpr/while/body/tkgn,nkd->tkgd/dot_general | solution.py:84
  47.3 2.0 %fusion.33 = f32[512,8]{0,1:T(8,128)S(1)} fusion(f32[512,512,8]{1,0,2:T(8,128)S(1)} %get-tuple-element.260, f32[512,8]{0,1:T(8,128)S(1)} %bitcast.107, pred[512,512]{0,1:T(8,128)(4,1)S(1)} %compare_and_fusion.2), kind=kLoop, calls=%fused_computation.5.clone.1 | loop fusion | flops 10481664 | bytes 8683520 | tf_op jit(solution)/shard_map/while/body/eval_jaxpr/while/body/reduce_sum | solution.py:83
  50.0 0.9 %compare_and_fusion.2 = pred[512,512]{0,1:T(8,128)(4,1)S(1)} fusion(s32[512]{0:T(512)S(1)} %get-tuple-element.256, s32[512]{0:T(512)} %get-tuple-element.295, s32[512]{0:T(512)S(1)} %get-tuple-element.257), kind=kLoop, calls=%fused_computation.12.clone.1 | loop fusion | flops 786432 | bytes 268288 | tf_op jit(solution)/shard_map/while/body/eval_jaxpr/while/body/and | solution.py:69
  51.0 2.4 %fusion.31 = (f32[512,8]{0,1:T(8,128)S(1)}, f32[512,512,8]{1,0,2:T(8,128)S(1)}) fusion(pred[512,512]{0,1:T(8,128)(4,1)S(1)} %compare_and_fusion.2, bf16[512,1,8,128]{3,0,2,1:T(8,128)(2,1)S(1)} %get-tuple-element.297, bf16[1536,1,128]{2,0,1:T(8,128)(2,1)} %get-tuple-element.296, s32[]{:T(128)S(6)} %select_n.64), kind=kOutput, calls=%fused_computation.3.clone.1 | convolution fusion | flops 543158272 | bytes 9846788 | tf_op jit(solution)/shard_map/while/body/eval_jaxpr/while/body/tkgd,nkd->tkgn/dot_general | solution.py:74
  53.4 3.7 %bitcast_add_fusion.5 = f32[512,1,8,128]{0,3,2,1:T(8,128)S(1)} fusion(f32[512,1,8,128]{0,3,2,1:T(8,128)S(1)} %get-tuple-element.279, f32[512,512,8]{1,0,2:T(8,128)S(1)} %get-tuple-element.260, f32[512,8]{0,1:T(8,128)S(1)} %bitcast.106, pred[512,512]{0,1:T(8,128)(4,1)S(1)} %compare_and_fusion.2, f32[512,8]{0,1:T(8,128)S(1)} %get-tuple-element.261, ...), kind=kOutput, calls=%fused_computation.9.clone.1 | convolution fusion | flops 548405248 | bytes 13008900 | tf_op jit(solution)/shard_map/while/body/eval_jaxpr/while/body/tkgn,nkd->tkgd/dot_general | solution.py:84
  57.1 2.0 %fusion.33 = f32[512,8]{0,1:T(8,128)S(1)} fusion(f32[512,512,8]{1,0,2:T(8,128)S(1)} %get-tuple-element.260, f32[512,8]{0,1:T(8,128)S(1)} %bitcast.107, pred[512,512]{0,1:T(8,128)(4,1)S(1)} %compare_and_fusion.2), kind=kLoop, calls=%fused_computation.5.clone.1 | loop fusion | flops 10481664 | bytes 8683520 | tf_op jit(solution)/shard_map/while/body/eval_jaxpr/while/body/reduce_sum | solution.py:83
  59.8 0.9 %compare_and_fusion.2 = pred[512,512]{0,1:T(8,128)(4,1)S(1)} fusion(s32[512]{0:T(512)S(1)} %get-tuple-element.256, s32[512]{0:T(512)} %get-tuple-element.295, s32[512]{0:T(512)S(1)} %get-tuple-element.257), kind=kLoop, calls=%fused_computation.12.clone.1 | loop fusion | flops 786432 | bytes 268288 | tf_op jit(solution)/shard_map/while/body/eval_jaxpr/while/body/and | solution.py:69
  60.8 2.4 %fusion.31 = (f32[512,8]{0,1:T(8,128)S(1)}, f32[512,512,8]{1,0,2:T(8,128)S(1)}) fusion(pred[512,512]{0,1:T(8,128)(4,1)S(1)} %compare_and_fusion.2, bf16[512,1,8,128]{3,0,2,1:T(8,128)(2,1)S(1)} %get-tuple-element.297, bf16[1536,1,128]{2,0,1:T(8,128)(2,1)} %get-tuple-element.296, s32[]{:T(128)S(6)} %select_n.64), kind=kOutput, calls=%fused_computation.3.clone.1 | convolution fusion | flops 543158272 | bytes 9846788 | tf_op jit(solution)/shard_map/while/body/eval_jaxpr/while/body/tkgd,nkd->tkgn/dot_general | solution.py:74
  63.2 3.7 %bitcast_add_fusion.5 = f32[512,1,8,128]{0,3,2,1:T(8,128)S(1)} fusion(f32[512,1,8,128]{0,3,2,1:T(8,128)S(1)} %get-tuple-element.279, f32[512,512,8]{1,0,2:T(8,128)S(1)} %get-tuple-element.260, f32[512,8]{0,1:T(8,128)S(1)} %bitcast.106, pred[512,512]{0,1:T(8,128)(4,1)S(1)} %compare_and_fusion.2, f32[512,8]{0,1:T(8,128)S(1)} %get-tuple-element.261, ...), kind=kOutput, calls=%fused_computation.9.clone.1 | convolution fusion | flops 548405248 | bytes 13008900 | tf_op jit(solution)/shard_map/while/body/eval_jaxpr/while/body/tkgn,nkd->tkgd/dot_general | solution.py:84
  67.0 2.0 %fusion.33 = f32[512,8]{0,1:T(8,128)S(1)} fusion(f32[512,512,8]{1,0,2:T(8,128)S(1)} %get-tuple-element.260, f32[512,8]{0,1:T(8,128)S(1)} %bitcast.107, pred[512,512]{0,1:T(8,128)(4,1)S(1)} %compare_and_fusion.2), kind=kLoop, calls=%fused_computation.5.clone.1 | loop fusion | flops 10481664 | bytes 8683520 | tf_op jit(solution)/shard_map/while/body/eval_jaxpr/while/body/reduce_sum | solution.py:83
  69.7 1.0 %divide_convert_fusion = bf16[512,1,8,128]{0,3,2,1:T(8,128)(2,1)S(1)} fusion(f32[512,1,8,128]{0,3,2,1:T(8,128)S(1)} %get-tuple-element.108, f32[512,8]{0,1:T(8,128)} %bitcast.112), kind=kLoop, calls=%fused_computation.28 | loop fusion | flops 1048576 | bytes 3162112 | tf_op jit(solution)/shard_map/while/body/eval_jaxpr/convert_element_type | solution.py:103
  71.6 17.1 %all_to_all.73 = bf16[4,128,1024]{2,1,0:T(8,128)(2,1)S(1)} all-to-all(bf16[4,128,1024]{2,1,0:T(8,128)(2,1)S(1)} %copy.32), channel_id=1, replica_groups=mesh['blk'=8,'uly'=4] {'uly'}, dimensions={0} | all-to-all | bytes 2097152 | tf_op jit(solution)/shard_map/all_to_all | solution.py:107
  89.4 1.3 %copy.30 = bf16[128,4096]{1,0:T(8,128)(2,1)} copy(bf16[128,4096]{0,1:T(8,128)(2,1)S(1)} %bitcast.110) | data formatting | bytes 2097152 | tf_op jit(solution)/shard_map/all_to_all | solution.py:107
  (39 shorter events, 5.6 us)
Async XLA Ops:
  0.0 5.0 %copy-start = (bf16[128,512]{1,0:T(8,128)(2,1)S(1)}, bf16[128,512]{1,0:T(8,128)(2,1)}, u32[]{:S(2)}) copy-start(bf16[128,512]{1,0:T(8,128)(2,1)} %param.7) | copy-start | bytes 393220
  1.7 7.9 %all-to-all-start.2 = ((bf16[128,4,128]{0,2,1:T(8,128)(2,1)}), bf16[128,4,128]{0,2,1:T(8,128)(2,1)S(1)}, u32[]{:S(2)}, u32[]{:S(2)}) async-start(bf16[128,4,128]{0,2,1:T(8,128)(2,1)} %bitcast.5), calls=%async_computation.2 | async-start | bytes 262144 | tf_op jit(solution)/shard_map/all_to_all | solution.py:32
  9.6 7.9 %all-to-all-start = ((bf16[128,4,128]{2,0,1:T(8,128)(2,1)}), bf16[128,4,128]{2,0,1:T(8,128)(2,1)S(1)}, u32[]{:S(2)}, u32[]{:S(2)}) async-start(bf16[128,4,128]{2,0,1:T(8,128)(2,1)} %copy_bitcast_fusion.1), calls=%async_computation | async-start | bytes 262144 | tf_op jit(solution)/shard_map/all_to_all | solution.py:31
  17.5 21.4 %all-to-all-start.1 = ((bf16[128,4,1024]{2,0,1:T(8,128)(2,1)}), bf16[128,4,1024]{2,0,1:T(8,128)(2,1)S(1)}, u32[]{:S(2)}, u32[]{:S(2)}) async-start(bf16[128,4,1024]{2,0,1:T(8,128)(2,1)} %bitcast.83), calls=%async_computation.1 | async-start | bytes 2097152 | tf_op jit(solution)/shard_map/all_to_all | solution.py:29
  21.2 11.6 %collective-permute-start.2 = (bf16[512,128]{1,0:T(8,128)(2,1)S(1)}, bf16[512,128]{1,0:T(8,128)(2,1)S(1)}, u32[]{:S(2)}, u32[]{:S(2)}) collective-permute-start(bf16[512,128]{1,0:T(8,128)(2,1)S(1)} %bitcast.116), channel_id=1, source_target_pairs={{0,8},{4,12},{8,16},{12,20},{16,24},{20,28},{1,9},{5,13},{9,17},{1... | collective-permute-start | bytes 393224 | tf_op jit(solution)/shard_map/ppermute | solution.py:15
  24.7 8.1 %collective-permute-start.3 = (bf16[512,128]{1,0:T(8,128)(2,1)S(1)}, bf16[512,128]{1,0:T(8,128)(2,1)S(1)}, u32[]{:S(2)}, u32[]{:S(2)}) collective-permute-start(bf16[512,128]{1,0:T(8,128)(2,1)S(1)} %bitcast.117), channel_id=1, source_target_pairs={{0,4},{4,8},{8,12},{12,16},{16,20},{20,24},{24,28},{1,5},{5,9},{9,... | collective-permute-start | bytes 393224 | tf_op jit(solution)/shard_map/ppermute | solution.py:15
  28.7 7.5 %collective-permute-start = (bf16[512,128]{1,0:T(8,128)(2,1)S(1)}, bf16[512,128]{1,0:T(8,128)(2,1)S(1)}, u32[]{:S(2)}, u32[]{:S(2)}) collective-permute-start(bf16[512,128]{1,0:T(8,128)(2,1)S(1)} %bitcast.113), channel_id=1, source_target_pairs={{0,8},{4,12},{8,16},{12,20},{16,24},{20,28},{1,9},{5,13},{9,17},{1... | collective-permute-start | bytes 393224 | tf_op jit(solution)/shard_map/ppermute | solution.py:15
  30.6 7.5 %collective-permute-start.1 = (bf16[512,128]{1,0:T(8,128)(2,1)S(1)}, bf16[512,128]{1,0:T(8,128)(2,1)S(1)}, u32[]{:S(2)}, u32[]{:S(2)}) collective-permute-start(bf16[512,128]{1,0:T(8,128)(2,1)S(1)} %bitcast.114), channel_id=1, source_target_pairs={{0,4},{4,8},{8,12},{12,16},{16,20},{20,24},{24,28},{1,5},{5,9},{9,... | collective-permute-start | bytes 393224 | tf_op jit(solution)/shard_map/ppermute | solution.py:15
  43.6 5.8 %copy-start.1 = (f32[512,1,8]{0,2,1:T(8,128)S(1)}, f32[512,1,8]{0,2,1:T(8,128)}, u32[]{:S(2)}) copy-start(f32[512,1,8]{0,2,1:T(8,128)} %get-tuple-element.278) | copy-start | bytes 49156 | tf_op jit(solution)/shard_map/while/body/eval_jaxpr/while
  49.4 0.6 copy-start.2
  53.4 5.8 %copy-start.1 = (f32[512,1,8]{0,2,1:T(8,128)S(1)}, f32[512,1,8]{0,2,1:T(8,128)}, u32[]{:S(2)}) copy-start(f32[512,1,8]{0,2,1:T(8,128)} %get-tuple-element.278) | copy-start | bytes 49156 | tf_op jit(solution)/shard_map/while/body/eval_jaxpr/while
  59.2 0.6 copy-start.2
  63.2 5.8 %copy-start.1 = (f32[512,1,8]{0,2,1:T(8,128)S(1)}, f32[512,1,8]{0,2,1:T(8,128)}, u32[]{:S(2)}) copy-start(f32[512,1,8]{0,2,1:T(8,128)} %get-tuple-element.278) | copy-start | bytes 49156 | tf_op jit(solution)/shard_map/while/body/eval_jaxpr/while
  69.0 0.6 copy-start.2
where the time goes:
time: 91.6 us; the launch traced here: 90.7 us
  starting transfers between devices  19.6 us (21%)
  matrix products  18.4 us (20%)
  blocking collectives  17.1 us (19%)
  other arithmetic  13 us (14%)
  local copies, waits for them, and re-layouts  10.8 us (12%)
  waiting for transfers between devices  10.7 us (12%)
    all_to_all x1, blocking collectives, local(): return lax.all_to_all(attn, 'uly', split_axis=0, concat_axis=1, tiled=True)  17.1 us
    dot_general x3, matrix products, add_tile(): jnp.einsum('tkgn,nkd->tkgd', exps.astype(jnp.bfloat16), value_tile, prefe...  11.2 us
    ppermute x4, starting transfers between devices, from_behind(): return lax.ppermute(block, axis, route)  9.44 us
    dot_general x3, matrix products, add_tile(): jnp.einsum('tkgd,nkd->tkgn', query_tile, key_tile, preferred_element_type...  7.21 us
    reduce_sum x3, other arithmetic, add_tile(): running_sum = running_sum * factor + jnp.sum(exps, axis=-1)  6.1 us
    ppermute x4, waiting for transfers between devices, from_behind(): return lax.ppermute(block, axis, route)  4.56 us
    all_to_all x1, waiting for transfers between devices, local(): lax.all_to_all(widen_heads(value_projection), 'uly', split_axis=1, concat...  3.88 us
    all_to_all x1, starting transfers between devices, local(): lax.all_to_all(query_projection, 'uly', split_axis=1, concat_axis=0, tile...  3.52 us
  transfers between devices with their start and end apart: 7, of which 4 were waited for; matrix products, arithmetic and copies ran while one was open for 7% of the time, Pallas kernels for 0%

commit v1 on v0

--- a/solution.py
+++ b/solution.py
@@ -7,6 +7,29 @@
 CYCLE_STEPS = 2
 POSITION_GROUP = 512
 masked_score = -1e30
+
+
+def in_blocks(value, dim, count):
+    shape = value.shape
+    tiles = value.reshape(*shape[:dim], count, shape[dim] // count, *shape[dim + 1 :])
+    return jnp.moveaxis(tiles, dim, 0)
+
+
+def laid_out(tiles, dim):
+    tiles = jnp.moveaxis(tiles, 0, dim)
+    lengths = tiles.shape
+    return tiles.reshape(*lengths[:dim], lengths[dim] * lengths[dim + 1], *lengths[dim + 2 :])
+
+
+def exchange_in_pairs(x, axis, split_dim, concat_dim):
+    count, position = (lax.axis_size(axis), lax.axis_index(axis))
+    blocks = in_blocks(x, split_dim, count)
+    done = [blocks[position]]
+    for step in range(1, count):
+        sent = blocks[position ^ step]
+        done.append(lax.ppermute(sent, axis, [(i, i ^ step) for i in range(count)]))
+    blocks = jnp.stack(done)[position ^ jnp.arange(count)]
+    return laid_out(blocks, concat_dim)
 
 
 def from_behind(block, axis, distance):
@@ -26,7 +49,7 @@
         copies = jnp.broadcast_to(split_heads, (tokens_dev, kv_heads, repeats, HEAD_WIDTH))
         return copies.reshape(tokens_dev, kv_heads * repeats * HEAD_WIDTH)
 
-    query_rows = lax.all_to_all(query_projection, "uly", split_axis=1, concat_axis=0, tiled=True)
+    query_rows = exchange_in_pairs(query_projection, "uly", 1, 0)
     key_rows, value_rows = (
         lax.all_to_all(widen_heads(key_projection), "uly", split_axis=1, concat_axis=0, tiled=True),
         lax.all_to_all(

time: 91.6 us -> 94.2 us (1.028)
  starting transfers between devices: 19.6 us -> 21.6 us
    all_to_all x1 -> x0, starting transfers between devices: 3.52 us -> none  [local(): lax.all_to_all(query_projection, 'uly', split_axis=1, concat_axis=0, tile...]
    all_to_all x1, waiting for transfers between devices: 3.88 us -> 7.38 us  [local(): lax.all_to_all(widen_heads(value_projection), 'uly', split_axis=1, concat...]
    ppermute x4, starting transfers between devices: 9.44 us -> 12.6 us  [from_behind(): return lax.ppermute(block, axis, route)]
    ppermute x0 -> x3, starting transfers between devices: none -> 2.34 us  [exchange_in_pairs(): done.append(lax.ppermute(sent, axis, [(i, i ^ step) for i in range(count)]))]
    all_to_all x1 -> x0, local copies, waits for them, and re-layouts: 2.29 us -> none  [local(): lax.all_to_all(query_projection, 'uly', split_axis=1, concat_axis=0, tile...]
    all_to_all x1, waiting for transfers between devices: 2.28 us -> 0.01 us  [local(): lax.all_to_all(widen_heads(key_projection), 'uly', split_axis=1, concat_a...]
    unnamed x5 -> x6, local copies, waits for them, and re-layouts: 2.11 us -> 3.71 us
    ppermute x4, waiting for transfers between devices: 4.56 us -> 3.02 us  [from_behind(): return lax.ppermute(block, axis, route)]
  transfers between devices with their start and end apart: 7 -> 9, of which waited for: 4 -> 3; matrix products, arithmetic and copies ran while one was open for 7% -> 6% of each run, Pallas kernels for 0% -> 0%
where the time goes in v1:
time: 94.2 us; the launch traced here: 93.4 us
  starting transfers between devices  21.6 us (23%)
  matrix products  18.4 us (20%)
  blocking collectives  17.5 us (19%)
  other arithmetic  13.1 us (14%)
  local copies, waits for them, and re-layouts  11.4 us (12%)
  waiting for transfers between devices  10.4 us (11%)
    all_to_all x1, blocking collectives, local(): return lax.all_to_all(attn, 'uly', split_axis=0, concat_axis=1, tiled=True)  17.5 us
    ppermute x4, starting transfers between devices, from_behind(): return lax.ppermute(block, axis, route)  12.6 us
    dot_general x3, matrix products, add_tile(): jnp.einsum('tkgn,nkd->tkgd', exps.astype(jnp.bfloat16), value_tile, prefe...  11.2 us
    all_to_all x1, waiting for transfers between devices, local(): lax.all_to_all(widen_heads(value_projection), 'uly', split_axis=1, concat...  7.38 us
    dot_general x3, matrix products, add_tile(): jnp.einsum('tkgd,nkd->tkgn', query_tile, key_tile, preferred_element_type...  7.21 us
    reduce_sum x3, other arithmetic, add_tile(): running_sum = running_sum * factor + jnp.sum(exps, axis=-1)  6.1 us
    unnamed x6, local copies, waits for them, and re-layouts  3.71 us
    all_to_all x1, starting transfers between devices, local(): lax.all_to_all(widen_heads(key_projection), 'uly', split_axis=1, concat_a...  3.33 us
  transfers between devices with their start and end apart: 9, of which 3 were waited for; matrix products, arithmetic and copies ran while one was open for 6% of the time, Pallas kernels for 0%

profile of v1, /device:TPU:18, one launch (start us, length us, event | category | flops | bytes accessed | tf_op | source)
XLA Modules:
  0.0 93.4 jit_solution(2708339761849453535)
XLA Ops:
  0.0 1.6 %copy.36 = bf16[128,4096]{0,1:T(8,128)(2,1)S(1)} copy(bf16[128,4096]{1,0:T(8,128)(2,1)} %param.6) | data formatting | bytes 2097152 | tf_op args[0]
  1.9 1.0 %collective-permute-start.4 = (bf16[128,1024]{1,0:T(8,128)(2,1)S(1)}, bf16[128,1024]{1,0:T(8,128)(2,1)S(1)}, u32[]{:S(2)}, u32[]{:S(2)}) collective-permute-start(bf16[128,1024]{1,0:T(8,128)(2,1)S(1)} %bitcast.125), channel_id=1, source_target_pairs={{0,3},{1,2},{2,1},{3,0},{4,7},{5,6},{6,5},{7,4},{8,11},{9,10},{10,... | collective-permute-start | bytes 786440 | tf_op jit(solution)/shard_map/ppermute | solution.py:30
  3.1 0.7 collective-permute-start.2
  4.6 1.7 %copy.41 = bf16[128,512]{0,1:T(8,128)(2,1)} copy(bf16[128,512]{1,0:T(8,128)(2,1)} %param.8) | data formatting | bytes 262144 | tf_op args[2]
  6.2 3.3 %all-to-all-start.1 = ((bf16[128,4,128]{0,2,1:T(8,128)(2,1)}), bf16[128,4,128]{0,2,1:T(8,128)(2,1)S(1)}, u32[]{:S(2)}, u32[]{:S(2)}) async-start(bf16[128,4,128]{0,2,1:T(8,128)(2,1)} %bitcast.13), calls=%async_computation.1 | async-start | bytes 262144 | tf_op jit(solution)/shard_map/all_to_all | solution.py:55
  9.5 0.7 copy_bitcast_fusion
  10.2 7.4 %all-to-all-done.1 = bf16[128,4,128]{0,2,1:T(8,128)(2,1)S(1)} async-done(((bf16[128,4,128]{0,2,1:T(8,128)(2,1)}), bf16[128,4,128]{0,2,1:T(8,128)(2,1)S(1)}, u32[]{:S(2)}, u32[]{:S(2)}) %all-to-all-start.1) | async-done | bytes 131104 | tf_op jit(solution)/shard_map/all_to_all | solution.py:55
  17.6 3.3 %all-to-all-start = ((bf16[128,4,128]{2,0,1:T(8,128)(2,1)}), bf16[128,4,128]{2,0,1:T(8,128)(2,1)S(1)}, u32[]{:S(2)}, u32[]{:S(2)}) async-start(bf16[128,4,128]{2,0,1:T(8,128)(2,1)} %copy_bitcast_fusion), calls=%async_computation | async-start | bytes 262144 | tf_op jit(solution)/shard_map/all_to_all | solution.py:54
  21.1 3.5 %collective-permute-start.5 = (bf16[512,128]{1,0:T(8,128)(2,1)S(1)}, bf16[512,128]{1,0:T(8,128)(2,1)S(1)}, u32[]{:S(2)}, u32[]{:S(2)}) collective-permute-start(bf16[512,128]{1,0:T(8,128)(2,1)S(1)} %bitcast.122), channel_id=1, source_target_pairs={{0,8},{4,12},{8,16},{12,20},{16,24},{20,28},{1,9},{5,13},{9,17},{1... | collective-permute-start | bytes 393224 | tf_op jit(solution)/shard_map/ppermute | solution.py:38
  24.6 1.9 %collective-permute-start.6 = (bf16[512,128]{1,0:T(8,128)(2,1)S(1)}, bf16[512,128]{1,0:T(8,128)(2,1)S(1)}, u32[]{:S(2)}, u32[]{:S(2)}) collective-permute-start(bf16[512,128]{1,0:T(8,128)(2,1)S(1)} %bitcast.123), channel_id=1, source_target_pairs={{0,4},{4,8},{8,12},{12,16},{16,20},{20,24},{24,28},{1,5},{5,9},{9,... | collective-permute-start | bytes 393224 | tf_op jit(solution)/shard_map/ppermute | solution.py:38
  26.5 1.3 %reduce_min.10 = s32[]{:T(128)} reduce(s32[512]{0:T(512)} %param.9, s32[]{:T(128)} %constant.101.clone.1), dimensions={0}, to_apply=%region_0.1 | reduce | flops 511 | bytes 2056 | tf_op jit(solution)/shard_map/while/body/eval_jaxpr/reduce_min | solution.py:83
  28.8 4.0 %collective-permute-start = (bf16[512,128]{1,0:T(8,128)(2,1)S(1)}, bf16[512,128]{1,0:T(8,128)(2,1)S(1)}, u32[]{:S(2)}, u32[]{:S(2)}) collective-permute-start(bf16[512,128]{1,0:T(8,128)(2,1)S(1)} %bitcast.119), channel_id=1, source_target_pairs={{0,8},{4,12},{8,16},{12,20},{16,24},{20,28},{1,9},{5,13},{9,17},{1... | collective-permute-start | bytes 393224 | tf_op jit(solution)/shard_map/ppermute | solution.py:38
  32.8 3.2 %collective-permute-start.1 = (bf16[512,128]{1,0:T(8,128)(2,1)S(1)}, bf16[512,128]{1,0:T(8,128)(2,1)S(1)}, u32[]{:S(2)}, u32[]{:S(2)}) collective-permute-start(bf16[512,128]{1,0:T(8,128)(2,1)S(1)} %bitcast.120), channel_id=1, source_target_pairs={{0,4},{4,8},{8,12},{12,16},{16,20},{20,24},{24,28},{1,5},{5,9},{9,... | collective-permute-start | bytes 393224 | tf_op jit(solution)/shard_map/ppermute | solution.py:38
  36.0 0.8 maximum_bitcast_fusion.1
  36.8 2.9 %collective-permute-done.1 = bf16[512,128]{1,0:T(8,128)(2,1)S(1)} collective-permute-done((bf16[512,128]{1,0:T(8,128)(2,1)S(1)}, bf16[512,128]{1,0:T(8,128)(2,1)S(1)}, u32[]{:S(2)}, u32[]{:S(2)}) %collective-permute-start.1) | collective-permute-done | bytes 131104 | tf_op jit(solution)/shard_map/ppermute | solution.py:38
  39.7 0.8 maximum_bitcast_fusion
  42.5 29.5 %while.24 = (s32[]{:T(128)}, f32[512,1,8]{0,2,1:T(8,128)S(1)}, f32[512,1,8]{0,2,1:T(8,128)}, f32[512,1,8,128]{0,3,2,1:T(8,128)S(1)}, s32[]{:T(128)}, /*index=5*/...) while((s32[]{:T(128)}, f32[512,1,8]{0,2,1:T(8,128)S(1)}, ...), condition=%wide.region_4.5_spmd.clone, body=%wide.region_1.4_spmd.clone.sunk | while | flops 1102853120 | bytes 32123144 | solution.py:123
  42.5 0.9 %compare_and_fusion.2 = pred[512,512]{0,1:T(8,128)(4,1)S(1)} fusion(s32[512]{0:T(512)S(1)} %get-tuple-element.270, s32[512]{0:T(512)} %get-tuple-element.309, s32[512]{0:T(512)S(1)} %get-tuple-element.271), kind=kLoop, calls=%fused_computation.13.clone.1 | loop fusion | flops 786432 | bytes 268288 | tf_op jit(solution)/shard_map/while/body/eval_jaxpr/while/body/and | solution.py:92
  43.5 2.4 %fusion.32 = (f32[512,8]{0,1:T(8,128)S(1)}, f32[512,512,8]{1,0,2:T(8,128)S(1)}) fusion(pred[512,512]{0,1:T(8,128)(4,1)S(1)} %compare_and_fusion.2, bf16[512,1,8,128]{3,0,2,1:T(8,128)(2,1)S(1)} %get-tuple-element.311, bf16[1536,1,128]{2,0,1:T(8,128)(2,1)} %get-tuple-element.310, s32[]{:T(128)S(6)} %select_n.94), kind=kOutput, calls=%fused_computation.4.clone.1 | convolution fusion | flops 543158272 | bytes 9846788 | tf_op jit(solution)/shard_map/while/body/eval_jaxpr/while/body/tkgd,nkd->tkgn/dot_general | solution.py:97
  45.9 3.7 %bitcast_add_fusion.5 = f32[512,1,8,128]{0,3,2,1:T(8,128)S(1)} fusion(f32[512,1,8,128]{0,3,2,1:T(8,128)S(1)} %get-tuple-element.293, f32[512,512,8]{1,0,2:T(8,128)S(1)} %get-tuple-element.274, f32[512,8]{0,1:T(8,128)S(1)} %bitcast.111, pred[512,512]{0,1:T(8,128)(4,1)S(1)} %compare_and_fusion.2, f32[512,8]{0,1:T(8,128)S(1)} %get-tuple-element.275, ...), kind=kOutput, calls=%fused_computation.10.clone.1 | convolution fusion | flops 548405248 | bytes 13008900 | tf_op jit(solution)/shard_map/while/body/eval_jaxpr/while/body/tkgn,nkd->tkgd/dot_general | solution.py:107
  49.7 2.0 %fusion.34 = f32[512,8]{0,1:T(8,128)S(1)} fusion(f32[512,512,8]{1,0,2:T(8,128)S(1)} %get-tuple-element.274, f32[512,8]{0,1:T(8,128)S(1)} %bitcast.112, pred[512,512]{0,1:T(8,128)(4,1)S(1)} %compare_and_fusion.2), kind=kLoop, calls=%fused_computation.6.clone.1 | loop fusion | flops 10481664 | bytes 8683520 | tf_op jit(solution)/shard_map/while/body/eval_jaxpr/while/body/reduce_sum | solution.py:106
  52.4 0.9 %compare_and_fusion.2 = pred[512,512]{0,1:T(8,128)(4,1)S(1)} fusion(s32[512]{0:T(512)S(1)} %get-tuple-element.270, s32[512]{0:T(512)} %get-tuple-element.309, s32[512]{0:T(512)S(1)} %get-tuple-element.271), kind=kLoop, calls=%fused_computation.13.clone.1 | loop fusion | flops 786432 | bytes 268288 | tf_op jit(solution)/shard_map/while/body/eval_jaxpr/while/body/and | solution.py:92
  53.3 2.4 %fusion.32 = (f32[512,8]{0,1:T(8,128)S(1)}, f32[512,512,8]{1,0,2:T(8,128)S(1)}) fusion(pred[512,512]{0,1:T(8,128)(4,1)S(1)} %compare_and_fusion.2, bf16[512,1,8,128]{3,0,2,1:T(8,128)(2,1)S(1)} %get-tuple-element.311, bf16[1536,1,128]{2,0,1:T(8,128)(2,1)} %get-tuple-element.310, s32[]{:T(128)S(6)} %select_n.94), kind=kOutput, calls=%fused_computation.4.clone.1 | convolution fusion | flops 543158272 | bytes 9846788 | tf_op jit(solution)/shard_map/while/body/eval_jaxpr/while/body/tkgd,nkd->tkgn/dot_general | solution.py:97
  55.8 3.7 %bitcast_add_fusion.5 = f32[512,1,8,128]{0,3,2,1:T(8,128)S(1)} fusion(f32[512,1,8,128]{0,3,2,1:T(8,128)S(1)} %get-tuple-element.293, f32[512,512,8]{1,0,2:T(8,128)S(1)} %get-tuple-element.274, f32[512,8]{0,1:T(8,128)S(1)} %bitcast.111, pred[512,512]{0,1:T(8,128)(4,1)S(1)} %compare_and_fusion.2, f32[512,8]{0,1:T(8,128)S(1)} %get-tuple-element.275, ...), kind=kOutput, calls=%fused_computation.10.clone.1 | convolution fusion | flops 548405248 | bytes 13008900 | tf_op jit(solution)/shard_map/while/body/eval_jaxpr/while/body/tkgn,nkd->tkgd/dot_general | solution.py:107
  59.5 2.0 %fusion.34 = f32[512,8]{0,1:T(8,128)S(1)} fusion(f32[512,512,8]{1,0,2:T(8,128)S(1)} %get-tuple-element.274, f32[512,8]{0,1:T(8,128)S(1)} %bitcast.112, pred[512,512]{0,1:T(8,128)(4,1)S(1)} %compare_and_fusion.2), kind=kLoop, calls=%fused_computation.6.clone.1 | loop fusion | flops 10481664 | bytes 8683520 | tf_op jit(solution)/shard_map/while/body/eval_jaxpr/while/body/reduce_sum | solution.py:106
  62.2 0.9 %compare_and_fusion.2 = pred[512,512]{0,1:T(8,128)(4,1)S(1)} fusion(s32[512]{0:T(512)S(1)} %get-tuple-element.270, s32[512]{0:T(512)} %get-tuple-element.309, s32[512]{0:T(512)S(1)} %get-tuple-element.271), kind=kLoop, calls=%fused_computation.13.clone.1 | loop fusion | flops 786432 | bytes 268288 | tf_op jit(solution)/shard_map/while/body/eval_jaxpr/while/body/and | solution.py:92
  63.1 2.4 %fusion.32 = (f32[512,8]{0,1:T(8,128)S(1)}, f32[512,512,8]{1,0,2:T(8,128)S(1)}) fusion(pred[512,512]{0,1:T(8,128)(4,1)S(1)} %compare_and_fusion.2, bf16[512,1,8,128]{3,0,2,1:T(8,128)(2,1)S(1)} %get-tuple-element.311, bf16[1536,1,128]{2,0,1:T(8,128)(2,1)} %get-tuple-element.310, s32[]{:T(128)S(6)} %select_n.94), kind=kOutput, calls=%fused_computation.4.clone.1 | convolution fusion | flops 543158272 | bytes 9846788 | tf_op jit(solution)/shard_map/while/body/eval_jaxpr/while/body/tkgd,nkd->tkgn/dot_general | solution.py:97
  65.6 3.7 %bitcast_add_fusion.5 = f32[512,1,8,128]{0,3,2,1:T(8,128)S(1)} fusion(f32[512,1,8,128]{0,3,2,1:T(8,128)S(1)} %get-tuple-element.293, f32[512,512,8]{1,0,2:T(8,128)S(1)} %get-tuple-element.274, f32[512,8]{0,1:T(8,128)S(1)} %bitcast.111, pred[512,512]{0,1:T(8,128)(4,1)S(1)} %compare_and_fusion.2, f32[512,8]{0,1:T(8,128)S(1)} %get-tuple-element.275, ...), kind=kOutput, calls=%fused_computation.10.clone.1 | convolution fusion | flops 548405248 | bytes 13008900 | tf_op jit(solution)/shard_map/while/body/eval_jaxpr/while/body/tkgn,nkd->tkgd/dot_general | solution.py:107
  69.3 2.0 %fusion.34 = f32[512,8]{0,1:T(8,128)S(1)} fusion(f32[512,512,8]{1,0,2:T(8,128)S(1)} %get-tuple-element.274, f32[512,8]{0,1:T(8,128)S(1)} %bitcast.112, pred[512,512]{0,1:T(8,128)(4,1)S(1)} %compare_and_fusion.2), kind=kLoop, calls=%fused_computation.6.clone.1 | loop fusion | flops 10481664 | bytes 8683520 | tf_op jit(solution)/shard_map/while/body/eval_jaxpr/while/body/reduce_sum | solution.py:106
  72.0 1.0 %divide_convert_fusion = bf16[512,1,8,128]{0,3,2,1:T(8,128)(2,1)S(1)} fusion(f32[512,1,8,128]{0,3,2,1:T(8,128)S(1)} %get-tuple-element.108, f32[512,8]{0,1:T(8,128)} %bitcast.118), kind=kLoop, calls=%fused_computation.29 | loop fusion | flops 1048576 | bytes 3162112 | tf_op jit(solution)/shard_map/while/body/eval_jaxpr/convert_element_type | solution.py:126
  74.0 17.5 %all_to_all.57 = bf16[4,128,1024]{2,1,0:T(8,128)(2,1)S(1)} all-to-all(bf16[4,128,1024]{2,1,0:T(8,128)(2,1)S(1)} %copy.49), channel_id=1, replica_groups=mesh['blk'=8,'uly'=4] {'uly'}, dimensions={0} | all-to-all | bytes 2097152 | tf_op jit(solution)/shard_map/all_to_all | solution.py:130
  92.1 1.3 %copy.47 = bf16[128,4096]{1,0:T(8,128)(2,1)} copy(bf16[128,4096]{0,1:T(8,128)(2,1)S(1)} %bitcast.116) | data formatting | bytes 2097152 | tf_op jit(solution)/shard_map/all_to_all | solution.py:130
  (52 shorter events, 7.0 us)
Async XLA Ops:
  0.0 9.5 %copy-start = (bf16[128,512]{1,0:T(8,128)(2,1)S(1)}, bf16[128,512]{1,0:T(8,128)(2,1)}, u32[]{:S(2)}) copy-start(bf16[128,512]{1,0:T(8,128)(2,1)} %param.7) | copy-start | bytes 393220
  1.9 38.6 %collective-permute-start.4 = (bf16[128,1024]{1,0:T(8,128)(2,1)S(1)}, bf16[128,1024]{1,0:T(8,128)(2,1)S(1)}, u32[]{:S(2)}, u32[]{:S(2)}) collective-permute-start(bf16[128,1024]{1,0:T(8,128)(2,1)S(1)} %bitcast.125), channel_id=1, source_target_pairs={{0,3},{1,2},{2,1},{3,0},{4,7},{5,6},{6,5},{7,4},{8,11},{9,10},{10,... | collective-permute-start | bytes 786440 | tf_op jit(solution)/shard_map/ppermute | solution.py:30
  3.1 37.4 %collective-permute-start.2 = (bf16[128,1024]{1,0:T(8,128)(2,1)S(1)}, bf16[128,1024]{1,0:T(8,128)(2,1)S(1)}, u32[]{:S(2)}, u32[]{:S(2)}) collective-permute-start(bf16[128,1024]{1,0:T(8,128)(2,1)S(1)} %bitcast.126), channel_id=1, source_target_pairs={{0,1},{1,0},{2,3},{3,2},{4,5},{5,4},{6,7},{7,6},{8,9},{9,8},{10,11... | collective-permute-start | bytes 786440 | tf_op jit(solution)/shard_map/ppermute | solution.py:30
  4.0 36.5 %collective-permute-start.3 = (bf16[128,1024]{1,0:T(8,128)(2,1)S(1)}, bf16[128,1024]{1,0:T(8,128)(2,1)S(1)}, u32[]{:S(2)}, u32[]{:S(2)}) collective-permute-start(bf16[128,1024]{1,0:T(8,128)(2,1)S(1)} %bitcast.127), channel_id=1, source_target_pairs={{0,2},{1,3},{2,0},{3,1},{4,6},{5,7},{6,4},{7,5},{8,10},{9,11},{10,... | collective-permute-start | bytes 786440 | tf_op jit(solution)/shard_map/ppermute | solution.py:30
  6.2 11.4 %all-to-all-start.1 = ((bf16[128,4,128]{0,2,1:T(8,128)(2,1)}), bf16[128,4,128]{0,2,1:T(8,128)(2,1)S(1)}, u32[]{:S(2)}, u32[]{:S(2)}) async-start(bf16[128,4,128]{0,2,1:T(8,128)(2,1)} %bitcast.13), calls=%async_computation.1 | async-start | bytes 262144 | tf_op jit(solution)/shard_map/all_to_all | solution.py:55
  17.6 11.1 %all-to-all-start = ((bf16[128,4,128]{2,0,1:T(8,128)(2,1)}), bf16[128,4,128]{2,0,1:T(8,128)(2,1)S(1)}, u32[]{:S(2)}, u32[]{:S(2)}) async-start(bf16[128,4,128]{2,0,1:T(8,128)(2,1)} %copy_bitcast_fusion), calls=%async_computation | async-start | bytes 262144 | tf_op jit(solution)/shard_map/all_to_all | solution.py:54
  21.1 7.8 %collective-permute-start.5 = (bf16[512,128]{1,0:T(8,128)(2,1)S(1)}, bf16[512,128]{1,0:T(8,128)(2,1)S(1)}, u32[]{:S(2)}, u32[]{:S(2)}) collective-permute-start(bf16[512,128]{1,0:T(8,128)(2,1)S(1)} %bitcast.122), channel_id=1, source_target_pairs={{0,8},{4,12},{8,16},{12,20},{16,24},{20,28},{1,9},{5,13},{9,17},{1... | collective-permute-start | bytes 393224 | tf_op jit(solution)/shard_map/ppermute | solution.py:38
  24.6 8.3 %collective-permute-start.6 = (bf16[512,128]{1,0:T(8,128)(2,1)S(1)}, bf16[512,128]{1,0:T(8,128)(2,1)S(1)}, u32[]{:S(2)}, u32[]{:S(2)}) collective-permute-start(bf16[512,128]{1,0:T(8,128)(2,1)S(1)} %bitcast.123), channel_id=1, source_target_pairs={{0,4},{4,8},{8,12},{12,16},{16,20},{20,24},{24,28},{1,5},{5,9},{9,... | collective-permute-start | bytes 393224 | tf_op jit(solution)/shard_map/ppermute | solution.py:38
  28.8 8.0 %collective-permute-start = (bf16[512,128]{1,0:T(8,128)(2,1)S(1)}, bf16[512,128]{1,0:T(8,128)(2,1)S(1)}, u32[]{:S(2)}, u32[]{:S(2)}) collective-permute-start(bf16[512,128]{1,0:T(8,128)(2,1)S(1)} %bitcast.119), channel_id=1, source_target_pairs={{0,8},{4,12},{8,16},{12,20},{16,24},{20,28},{1,9},{5,13},{9,17},{1... | collective-permute-start | bytes 393224 | tf_op jit(solution)/shard_map/ppermute | solution.py:38
  32.8 6.9 %collective-permute-start.1 = (bf16[512,128]{1,0:T(8,128)(2,1)S(1)}, bf16[512,128]{1,0:T(8,128)(2,1)S(1)}, u32[]{:S(2)}, u32[]{:S(2)}) collective-permute-start(bf16[512,128]{1,0:T(8,128)(2,1)S(1)} %bitcast.120), channel_id=1, source_target_pairs={{0,4},{4,8},{8,12},{12,16},{16,20},{20,24},{24,28},{1,5},{5,9},{9,... | collective-permute-start | bytes 393224 | tf_op jit(solution)/shard_map/ppermute | solution.py:38
  45.9 5.8 %copy-start.1 = (f32[512,1,8]{0,2,1:T(8,128)S(1)}, f32[512,1,8]{0,2,1:T(8,128)}, u32[]{:S(2)}) copy-start(f32[512,1,8]{0,2,1:T(8,128)} %get-tuple-element.292) | copy-start | bytes 49156 | tf_op jit(solution)/shard_map/while/body/eval_jaxpr/while
  51.8 0.6 copy-start.2
  55.8 5.8 %copy-start.1 = (f32[512,1,8]{0,2,1:T(8,128)S(1)}, f32[512,1,8]{0,2,1:T(8,128)}, u32[]{:S(2)}) copy-start(f32[512,1,8]{0,2,1:T(8,128)} %get-tuple-element.292) | copy-start | bytes 49156 | tf_op jit(solution)/shard_map/while/body/eval_jaxpr/while
  61.6 0.6 copy-start.2
  65.6 5.8 %copy-start.1 = (f32[512,1,8]{0,2,1:T(8,128)S(1)}, f32[512,1,8]{0,2,1:T(8,128)}, u32[]{:S(2)}) copy-start(f32[512,1,8]{0,2,1:T(8,128)} %get-tuple-element.292) | copy-start | bytes 49156 | tf_op jit(solution)/shard_map/while/body/eval_jaxpr/while
  71.4 0.6 copy-start.2
